TPU v7x, 512 devices: a whole 4x8x8 slice. The times are simulated.
512 devices in a mesh: depth: 64 (over z_lo, y, core), cols: 8 (over x, z_hi).
Axes of the slice: x: 4, y: 8, z: 8 (z_hi: 2, z_lo: 4; z = z_hi * 4 + z_lo), core: 2. Of those that a mesh axis runs over, the one named last changes fastest.
Arguments:
- field: float32 [128, 2048, 1024], P('depth', None, 'cols'), may hold values from -6 to 6
Outputs:
- picture: float32 [4, 2048, 1024], P(None, 'depth', 'cols')
All inputs are finite; a program needn't handle non-finite values.
Results may differ from a plain program's by a relative error of at most 0.00002.
Values sent between devices are 32-bit elements; how exact they have to be, the bound alone decides.
A program may use at most 128 MiB of HBM per device.

v0:
```python
import math

import jax
import jax.numpy as jnp
from jax import lax
from jax.sharding import PartitionSpec as P


def extended(shard, sides, width):
    for axis, dim in sides:
        size, length = (lax.axis_size(axis), shard.shape[dim])
        up = [(i, (i + 1) % size) for i in range(size - 1)]
        down = [(j, i) for i, j in up]
        last = lax.slice_in_dim(shard, length - width, length, axis=dim)
        initial = lax.slice_in_dim(shard, 0, width, axis=dim)
        before = lax.ppermute(last, axis, up)
        after = lax.ppermute(initial, axis, down)
        shard = jnp.concatenate([before, shard, after], axis=dim)
    return shard


def swapped(block, axis, bit):
    count = lax.axis_size(axis)
    route = []
    for low in range(count):
        high = low | 1 << bit
        if high != low and high < count:
            route += [(low, high), (high, low)]
    return lax.ppermute(block, axis, route)


def apply_taps(array_in, tap_list, which_axis):
    length = array_in.shape[which_axis] - 4
    result = tap_list[0] * lax.slice_in_dim(array_in, 0, length, axis=which_axis)
    for offset in range(1, 5):
        result = result + tap_list[offset] * lax.slice_in_dim(
            array_in, offset, offset + length, axis=which_axis
        )
    return result


def render_slab(padded):
    gauss_taps = [1.0 / 16, 4.0 / 16, 6.0 / 16, 4.0 / 16, 1.0 / 16]
    deriv_taps = [-1.0 / 8, -2.0 / 8, 0.0, 2.0 / 8, 1.0 / 8]
    smooth_x = apply_taps(padded, gauss_taps, 2)
    deriv_x = apply_taps(padded, deriv_taps, 2)
    smooth_xy = apply_taps(smooth_x, gauss_taps, 1)
    deriv_y = apply_taps(smooth_x, deriv_taps, 1)
    deriv_xy = apply_taps(deriv_x, gauss_taps, 1)
    smooth = apply_taps(smooth_xy, gauss_taps, 0)
    grad_z = 8.0 * apply_taps(smooth_xy, deriv_taps, 0)
    grad_y = 8.0 * apply_taps(deriv_y, gauss_taps, 0)
    grad_x = 8.0 * apply_taps(deriv_xy, gauss_taps, 0)
    scaled = 7.0 * smooth
    opacity = 0.6 * jax.nn.sigmoid(6.0 * scaled - 13.2)
    norm_len = jnp.sqrt(grad_x * grad_x + grad_y * grad_y + grad_z * grad_z + 1.0)
    half_len = math.sqrt(0.48 * 0.48 + 0.6 * 0.6 + 1.64 * 1.64)
    dot_light = (0.48 * grad_x + 0.6 * grad_y + 0.64 * grad_z) / norm_len
    dot_half = (0.48 * grad_x + 0.6 * grad_y + 1.64 * grad_z) / (half_len * norm_len)
    shading = 0.25 + 0.6 * jnp.maximum(dot_light, 0.0) + 0.35 * jnp.maximum(dot_half, 0.0) ** 8
    weight = opacity * shading
    colours = jnp.stack(
        [
            jax.nn.sigmoid(2.0 * scaled + 0.5) * weight,
            (0.5 + 0.4 * jnp.tanh(scaled)) * weight,
            jax.nn.sigmoid(-2.0 * scaled) * weight,
        ],
        0,
    )
    return (colours, opacity)


def composite_planes(colours, opacity):

    def step_fn(state_pair, plane):
        colour_sum, opacity_sum = state_pair
        plane_colour, plane_opacity = plane
        remain = 1.0 - opacity_sum
        return (
            (colour_sum + remain[None] * plane_colour, opacity_sum + remain * plane_opacity),
            None,
        )

    start = (
        jnp.zeros(colours.shape[0:1] + colours.shape[2:], jnp.float32),
        jnp.zeros(opacity.shape[1:], jnp.float32),
    )
    final_pair, unused = lax.scan(step_fn, start, (jnp.moveaxis(colours, 1, 0), opacity))
    return jnp.concatenate([final_pair[0], final_pair[1][None]], 0)


def over_op(front_part, back_part):
    return front_part + (1.0 - front_part[3:4]) * back_part


def local(field):
    widened = extended(field, (("depth", 0), ("cols", 2)), 2)
    padded = jnp.pad(widened, ((0, 0), (2, 2), (0, 0)))
    colours, opacity = render_slab(padded)
    partial_image = composite_planes(colours, opacity)
    groups = lax.axis_size("depth")
    position = lax.axis_index("depth")
    section_count = groups.bit_length() - 1
    block_rows = partial_image.shape[1] // groups
    current = partial_image.reshape(4, groups, block_rows, partial_image.shape[2])
    for bit_num in range(section_count):
        lower = current[:, 0::2]
        upper = current[:, 1::2]
        upper_side = position // 2**bit_num % 2 == 1
        kept = jnp.where(upper_side, upper, lower)
        outgoing = jnp.where(upper_side, lower, upper)
        incoming = swapped(outgoing, "depth", bit_num)
        front_part = jnp.where(upper_side, incoming, kept)
        back_part = jnp.where(upper_side, kept, incoming)
        current = over_op(front_part, back_part)
    return current[:, 0]


def solution(mesh):
    return jax.shard_map(
        local,
        mesh=mesh,
        in_specs=(P("depth", None, "cols"),),
        out_specs=P(None, "depth", "cols"),
        check_vma=False,
    )
```

profile of v0, /device:TPU:6, one launch (start us, length us, event | category | flops | bytes accessed | tf_op | source)
XLA Modules:
  0.0 262.9 jit_solution(8658273243053690812)
XLA Ops:
  5.1 2.3 collective-permute-done
  7.4 3.6 %collective-permute-done.1 = f32[2,2048,128]{1,2,0:T(8,128)S(1)} collective-permute-done((f32[2,2048,128]{1,2,0:T(8,128)S(1)}, f32[2,2048,128]{1,2,0:T(8,128)S(1)}, u32[]{:S(2)}, u32[]{:S(2)}) %collective-permute-start.1) | collective-permute-done | bytes 2097184 | tf_op jit(solution)/shard_map/ppermute | solution.py:17
  12.4 10.9 %collective-permute-start.2 = (f32[6,2048,2]{1,2,0:T(2,128)S(1)}, f32[6,2048,2]{1,2,0:T(2,128)S(1)}, u32[]{:S(2)}, u32[]{:S(2)}) collective-permute-start(f32[6,2048,2]{1,2,0:T(2,128)S(1)} %get-tuple-element.88), channel_id=1, source_target_pairs={{0,1},{1,2},{2,3},{3,4},{4,5},{5,6},{6,7},{8,9},{9,10},{10,11},{11... | collective-permute-start | bytes 294920 | tf_op jit(solution)/shard_map/ppermute | solution.py:16
  23.3 2.2 collective-permute-start.3
  25.6 15.6 %collective-permute-done.2 = f32[6,2048,2]{1,2,0:T(2,128)S(1)} collective-permute-done((f32[6,2048,2]{1,2,0:T(2,128)S(1)}, f32[6,2048,2]{1,2,0:T(2,128)S(1)}, u32[]{:S(2)}, u32[]{:S(2)}) %collective-permute-start.2) | collective-permute-done | bytes 98336 | tf_op jit(solution)/shard_map/ppermute | solution.py:16
  41.2 8.2 %select_maximum_fusion = f32[6,2052,132]{1,2,0:T(8,128)S(1)} fusion(f32[6,2048,2]{1,2,0:T(2,128)S(1)} %collective-permute-done.3, f32[6,2048,2]{1,2,0:T(2,128)S(1)} %collective-permute-done.2, f32[2,2048,128]{1,2,0:T(8,128)} %copy-done.5, f32[2,2048,128]{1,2,0:T(8,128)S(1)} %copy.4, f32[2,2048,128]{1,2,0:T(8,128)} %copy-done.4), kind=kLoop, calls=%fused_computation.9 | loop fusion | flops 19502208 | bytes 12988800 | tf_op jit(solution)/shard_map/concatenate | solution.py:18
  49.4 6.8 %multiply_add_fusion = (f32[6,2052,128]{1,2,0:T(8,128)S(1)}, f32[6,2052,128]{1,2,0:T(8,128)}) fusion(f32[6,2052,132]{1,2,0:T(8,128)S(1)} %select_maximum_fusion), kind=kLoop, calls=%fused_computation.15 | loop fusion | flops 26790912 | bytes 44126208 | tf_op jit(solution)/shard_map/add | solution.py:36
  56.2 20.0 %multiply_add_fusion.2 = (f32[6,2048,128]{1,2,0:T(8,128)}, f32[6,2048,128]{1,2,0:T(8,128)}) fusion(f32[6,2052,128]{1,2,0:T(8,128)} %get-tuple-element.85), kind=kLoop, calls=%fused_computation.28 | loop fusion | flops 26738688 | bytes 44040192 | tf_op jit(solution)/shard_map/add | solution.py:36
  76.2 6.8 %divide_multiply_fusion = (f32[2,2048,128]{1,2,0:T(8,128)}, f32[2,2048,128]{1,2,0:T(8,128)S(1)}) fusion(f32[6,2048,128]{1,2,0:T(8,128)} %get-tuple-element.87), kind=kLoop, calls=%fused_computation.55 | loop fusion | flops 7864320 | bytes 14680064 | tf_op jit(solution)/shard_map/mul | solution.py:55
  83.0 8.3 %fusion.3 = f32[6,2048,128]{1,2,0:T(8,128)} fusion(f32[6,2052,128]{1,2,0:T(8,128)S(1)} %get-tuple-element.84), kind=kLoop, calls=%fused_computation.18 | loop fusion | flops 14155776 | bytes 37748736 | tf_op jit(solution)/shard_map/add | solution.py:36
  91.3 10.7 %multiply_bitcast_fusion.2 = (f32[1,2,2048,128]{2,3,1,0:T(8,128)S(1)}, f32[2,2048,128]{1,2,0:T(8,128)S(1)}) fusion(f32[2,2048,128]{1,2,0:T(8,128)S(1)} %get-tuple-element.79, f32[6,2048,128]{1,2,0:T(8,128)S(1)} %bitcast.37, f32[6,2048,128]{1,2,0:T(8,128)} %get-tuple-element.86, f32[6,2048,128]{1,2,0:T(8,128)} %fusion.3), kind=kLoop, calls=%fused_computation.53 | loop fusion | flops 35651584 | bytes 37748736 | tf_op jit(solution)/shard_map/stack | solution.py:62
  102.8 3.1 %maximum_bitcast_fusion = f32[2,3,2048,128]{2,3,0,1:T(8,128)} fusion(f32[1,2,2048,128]{2,3,1,0:T(8,128)S(1)} %get-tuple-element.91, f32[1,2,2048,128]{2,3,1,0:T(8,128)S(1)} %get-tuple-element.90, f32[1,2,2048,128]{2,3,1,0:T(8,128)S(1)} %get-tuple-element.80), kind=kLoop, calls=%fused_computation.27 | loop fusion | flops 3145728 | bytes 12582912 | tf_op jit(solution)/shard_map/transpose | solution.py:88
  105.9 27.5 %while.13 = (s32[]{:T(128)}, f32[3,2048,128]{2,1,0:T(8,128)}, f32[2048,128]{1,0:T(8,128)S(1)}, f32[2,3,2048,128]{2,3,0,1:T(8,128)}, f32[2,2048,128]{1,2,0:T(8,128)}, /*index=5*/s32[]{:T(128)}, s32[]{:T(128)}) while((s32[]{:T(128)}, f32[3,2048,128]{2,1,0:T(8,128)}, f32[2048,128]{1,0:T(8,128)S(1)}, f32[2,3,2048,128]{2,3,0,1:T(8,128)}, ...), condition=%wide.region_1.2_spmd.clone, body=%wide.region_0.1_spmd.clone.sunk | while | flops 3407875 | bytes 39846036 | solution.py:88
  112.5 2.4 copy.13
  114.9 4.3 %fusion.24 = f32[3,2048,128]{2,1,0:T(8,128)} fusion(f32[1,3,2048,128]{3,2,1,0:T(8,128)} %copy.13, f32[3,2048,128]{2,1,0:T(8,128)} %get-tuple-element.135, f32[2048,128]{1,0:T(8,128)} %get-tuple-element.125, pred[]{:T(512)S(6)} %compare.39), kind=kLoop, calls=%fused_computation.1.clone.1 | loop fusion | flops 2359296 | bytes 10485761 | tf_op jit(solution)/shard_map/while/body/eval_jaxpr/add | solution.py:80
  125.8 2.4 copy.13
  128.2 5.2 %fusion.24 = f32[3,2048,128]{2,1,0:T(8,128)} fusion(f32[1,3,2048,128]{3,2,1,0:T(8,128)} %copy.13, f32[3,2048,128]{2,1,0:T(8,128)} %get-tuple-element.135, f32[2048,128]{1,0:T(8,128)} %get-tuple-element.125, pred[]{:T(512)S(6)} %compare.39), kind=kLoop, calls=%fused_computation.1.clone.1 | loop fusion | flops 2359296 | bytes 10485761 | tf_op jit(solution)/shard_map/while/body/eval_jaxpr/add | solution.py:80
  133.4 2.5 pad_maximum_fusion
  136.0 2.2 slice_select_fusion.1
  138.6 15.2 %collective-permute-start.4 = (f32[4,32,32,128]{3,2,1,0:T(8,128)}, f32[4,32,32,128]{3,2,1,0:T(8,128)S(1)}, u32[]{:S(2)}, u32[]{:S(2)}) collective-permute-start(f32[4,32,32,128]{3,2,1,0:T(8,128)} %slice_select_fusion.1), channel_id=1, source_target_pairs={{0,8},{8,0},{16,24},{24,16},{32,40},{40,32},{48,56},{56,48},{64,72... | collective-permute-start | bytes 6291464 | tf_op jit(solution)/shard_map/ppermute | solution.py:29
  153.8 3.7 %collective-permute-done.4 = f32[4,32,32,128]{3,2,1,0:T(8,128)S(1)} collective-permute-done((f32[4,32,32,128]{3,2,1,0:T(8,128)}, f32[4,32,32,128]{3,2,1,0:T(8,128)S(1)}, u32[]{:S(2)}, u32[]{:S(2)}) %collective-permute-start.4) | collective-permute-done | bytes 2097184 | tf_op jit(solution)/shard_map/ppermute | solution.py:29
  157.5 3.8 %broadcast_select_fusion = f32[4,32,32,128]{3,2,1,0:T(8,128)S(1)} fusion(f32[4,32,32,128]{3,2,1,0:T(8,128)S(1)} %collective-permute-done.4, pred[]{:T(512)S(6)} %eq.30, f32[4,64,32,128]{3,2,1,0:T(8,128)} %copy-done), kind=kLoop, calls=%fused_computation.60 | loop fusion | flops 1048576 | bytes 8388609 | tf_op jit(solution)/shard_map/jit(_where)/select_n | solution.py:113
  161.8 2.4 multiply_add_fusion.4
  165.4 8.0 %collective-permute-start.5 = (f32[4,16,32,128]{3,2,1,0:T(8,128)}, f32[4,16,32,128]{3,2,1,0:T(8,128)S(1)}, u32[]{:S(2)}, u32[]{:S(2)}) collective-permute-start(f32[4,16,32,128]{3,2,1,0:T(8,128)} %slice_select_fusion.3), channel_id=1, source_target_pairs={{0,16},{16,0},{8,24},{24,8},{32,48},{48,32},{40,56},{56,40},{64,80... | collective-permute-start | bytes 3145736 | tf_op jit(solution)/shard_map/ppermute | solution.py:29
  173.4 23.9 %collective-permute-done.5 = f32[4,16,32,128]{3,2,1,0:T(8,128)S(1)} collective-permute-done((f32[4,16,32,128]{3,2,1,0:T(8,128)}, f32[4,16,32,128]{3,2,1,0:T(8,128)S(1)}, u32[]{:S(2)}, u32[]{:S(2)}) %collective-permute-start.5) | collective-permute-done | bytes 1048608 | tf_op jit(solution)/shard_map/ppermute | solution.py:29
  200.0 4.7 %collective-permute-start.6 = (f32[4,8,32,128]{3,2,1,0:T(8,128)S(1)}, f32[4,8,32,128]{3,2,1,0:T(8,128)S(1)}, u32[]{:S(2)}, u32[]{:S(2)}) collective-permute-start(f32[4,8,32,128]{3,2,1,0:T(8,128)S(1)} %slice_select_fusion.5), channel_id=1, source_target_pairs={{0,32},{32,0},{8,40},{40,8},{16,48},{48,16},{24,56},{56,24},{64,96... | collective-permute-start | bytes 1572872 | tf_op jit(solution)/shard_map/ppermute | solution.py:29
  204.7 23.0 %collective-permute-done.6 = f32[4,8,32,128]{3,2,1,0:T(8,128)S(1)} collective-permute-done((f32[4,8,32,128]{3,2,1,0:T(8,128)S(1)}, f32[4,8,32,128]{3,2,1,0:T(8,128)S(1)}, u32[]{:S(2)}, u32[]{:S(2)}) %collective-permute-start.6) | collective-permute-done | bytes 524320 | tf_op jit(solution)/shard_map/ppermute | solution.py:29
  228.0 7.7 %collective-permute-start.7 = (f32[4,4,32,128]{3,2,1,0:T(8,128)S(1)}, f32[4,4,32,128]{3,2,1,0:T(8,128)S(1)}, u32[]{:S(2)}, u32[]{:S(2)}) collective-permute-start(f32[4,4,32,128]{3,2,1,0:T(8,128)S(1)} %slice_select_fusion.7), channel_id=1, source_target_pairs={{0,64},{64,0},{8,72},{72,8},{16,80},{80,16},{24,88},{88,24},{32,96... | collective-permute-start | bytes 786440 | tf_op jit(solution)/shard_map/ppermute | solution.py:29
  235.7 12.1 %collective-permute-done.7 = f32[4,4,32,128]{3,2,1,0:T(8,128)S(1)} collective-permute-done((f32[4,4,32,128]{3,2,1,0:T(8,128)S(1)}, f32[4,4,32,128]{3,2,1,0:T(8,128)S(1)}, u32[]{:S(2)}, u32[]{:S(2)}) %collective-permute-start.7) | collective-permute-done | bytes 262176 | tf_op jit(solution)/shard_map/ppermute | solution.py:29
  250.0 4.9 %collective-permute-done.8 = f32[4,2,32,128]{3,2,1,0:T(8,128)S(1)} collective-permute-done((f32[4,2,32,128]{3,2,1,0:T(8,128)S(1)}, f32[4,2,32,128]{3,2,1,0:T(8,128)S(1)}, u32[]{:S(2)}, u32[]{:S(2)}) %collective-permute-start.8) | collective-permute-done | bytes 131104 | tf_op jit(solution)/shard_map/ppermute | solution.py:29
  255.0 2.2 collective-permute-start.9
  257.2 5.0 %collective-permute-done.9 = f32[4,1,32,128]{3,2,1,0:T(8,128)S(1)} collective-permute-done((f32[4,1,32,128]{3,2,1,0:T(8,128)S(1)}, f32[4,1,32,128]{3,2,1,0:T(8,128)S(1)}, u32[]{:S(2)}, u32[]{:S(2)}) %collective-permute-start.9) | collective-permute-done | bytes 65568 | tf_op jit(solution)/shard_map/ppermute | solution.py:29
  (63 shorter events, 28.4 us)
Async XLA Ops:
  1.9 5.5 %collective-permute-start = (f32[2,2048,128]{1,2,0:T(8,128)S(1)}, f32[2,2048,128]{1,2,0:T(8,128)S(1)}, u32[]{:S(2)}, u32[]{:S(2)}) collective-permute-start(f32[2,2048,128]{1,2,0:T(8,128)S(1)} %copy.4), channel_id=1, source_target_pairs={{0,8},{8,16},{16,24},{24,32},{32,40},{40,48},{48,56},{56,64},{64,7... | collective-permute-start | bytes 6291464 | tf_op jit(solution)/shard_map/ppermute | solution.py:16
  3.8 7.3 %collective-permute-start.1 = (f32[2,2048,128]{1,2,0:T(8,128)S(1)}, f32[2,2048,128]{1,2,0:T(8,128)S(1)}, u32[]{:S(2)}, u32[]{:S(2)}) collective-permute-start(f32[2,2048,128]{1,2,0:T(8,128)S(1)} %copy.4), channel_id=1, source_target_pairs={{8,0},{16,8},{24,16},{32,24},{40,32},{48,40},{56,48},{64,56},{72,6... | collective-permute-start | bytes 6291464 | tf_op jit(solution)/shard_map/ppermute | solution.py:17
  7.4 3.7 %copy-start.4 = (f32[2,2048,128]{1,2,0:T(8,128)}, f32[2,2048,128]{1,2,0:T(8,128)S(1)}, u32[]{:S(2)}) copy-start(f32[2,2048,128]{1,2,0:T(8,128)S(1)} %collective-permute-done) | copy-start | bytes 6291460
  11.1 1.3 copy-start.5
  12.4 28.8 %collective-permute-start.2 = (f32[6,2048,2]{1,2,0:T(2,128)S(1)}, f32[6,2048,2]{1,2,0:T(2,128)S(1)}, u32[]{:S(2)}, u32[]{:S(2)}) collective-permute-start(f32[6,2048,2]{1,2,0:T(2,128)S(1)} %get-tuple-element.88), channel_id=1, source_target_pairs={{0,1},{1,2},{2,3},{3,4},{4,5},{5,6},{6,7},{8,9},{9,10},{10,11},{11... | collective-permute-start | bytes 294920 | tf_op jit(solution)/shard_map/ppermute | solution.py:16
  23.3 17.8 %collective-permute-start.3 = (f32[6,2048,2]{1,2,0:T(2,128)S(1)}, f32[6,2048,2]{1,2,0:T(2,128)S(1)}, u32[]{:S(2)}, u32[]{:S(2)}) collective-permute-start(f32[6,2048,2]{1,2,0:T(2,128)S(1)} %get-tuple-element.89), channel_id=1, source_target_pairs={{1,0},{2,1},{3,2},{4,3},{5,4},{6,5},{7,6},{9,8},{10,9},{11,10},{12... | collective-permute-start | bytes 294920 | tf_op jit(solution)/shard_map/ppermute | solution.py:17
  83.0 8.3 %slice-start = ((s8[6291456]{0:T(1024)(128)(4,1)}), s8[4194304]{0:T(1024)(128)(4,1)S(1)}, s32[]{:S(2)}) async-start(s8[6291456]{0:T(1024)(128)(4,1)} %bitcast.36), calls=%async_computation | async-start | bytes 8388608
  83.0 8.3 %slice-start.1 = ((s8[6291456]{0:T(1024)(128)(4,1)}), s8[2097152]{0:T(1024)(128)(4,1)S(1)}, s32[]{:S(2)}) async-start(s8[6291456]{0:T(1024)(128)(4,1)} %bitcast.36), calls=%async_computation.1 | async-start | bytes 4194304
  109.4 1.0 copy-start.2
  114.9 4.3 %copy-start.3 = (f32[2048,128]{1,0:T(8,128)S(1)}, f32[2048,128]{1,0:T(8,128)}, u32[]{:S(2)}) copy-start(f32[2048,128]{1,0:T(8,128)} %copy-done.2) | copy-start | bytes 3145732 | tf_op jit(solution)/shard_map/while
  122.7 1.0 copy-start.2
  128.2 5.2 %copy-start.3 = (f32[2048,128]{1,0:T(8,128)S(1)}, f32[2048,128]{1,0:T(8,128)}, u32[]{:S(2)}) copy-start(f32[2048,128]{1,0:T(8,128)} %copy-done.2) | copy-start | bytes 3145732 | tf_op jit(solution)/shard_map/while
  136.0 2.6 %copy-start = (f32[4,64,32,128]{3,2,1,0:T(8,128)}, f32[4,64,32,128]{3,2,1,0:T(8,128)S(1)}, u32[]{:S(2)}) copy-start(f32[4,64,32,128]{3,2,1,0:T(8,128)S(1)} %pad_maximum_fusion) | copy-start | bytes 12582916
  138.6 18.9 %collective-permute-start.4 = (f32[4,32,32,128]{3,2,1,0:T(8,128)}, f32[4,32,32,128]{3,2,1,0:T(8,128)S(1)}, u32[]{:S(2)}, u32[]{:S(2)}) collective-permute-start(f32[4,32,32,128]{3,2,1,0:T(8,128)} %slice_select_fusion.1), channel_id=1, source_target_pairs={{0,8},{8,0},{16,24},{24,16},{32,40},{40,32},{48,56},{56,48},{64,72... | collective-permute-start | bytes 6291464 | tf_op jit(solution)/shard_map/ppermute | solution.py:29
  157.5 3.8 %copy-start.6 = (f32[4,32,32,128]{3,2,1,0:T(8,128)}, f32[4,32,32,128]{3,2,1,0:T(8,128)S(1)}, u32[]{:S(2)}) copy-start(f32[4,32,32,128]{3,2,1,0:T(8,128)S(1)} %collective-permute-done.4) | copy-start | bytes 6291460
  157.5 4.2 %copy-start.1 = (f32[4,64,32,128]{3,2,1,0:T(8,128)S(1)}, f32[4,64,32,128]{3,2,1,0:T(8,128)}, u32[]{:S(2)}) copy-start(f32[4,64,32,128]{3,2,1,0:T(8,128)} %copy-done) | copy-start | bytes 12582916
  165.4 31.9 %collective-permute-start.5 = (f32[4,16,32,128]{3,2,1,0:T(8,128)}, f32[4,16,32,128]{3,2,1,0:T(8,128)S(1)}, u32[]{:S(2)}, u32[]{:S(2)}) collective-permute-start(f32[4,16,32,128]{3,2,1,0:T(8,128)} %slice_select_fusion.3), channel_id=1, source_target_pairs={{0,16},{16,0},{8,24},{24,8},{32,48},{48,32},{40,56},{56,40},{64,80... | collective-permute-start | bytes 3145736 | tf_op jit(solution)/shard_map/ppermute | solution.py:29
  197.2 1.0 copy-start.7
  200.0 27.7 %collective-permute-start.6 = (f32[4,8,32,128]{3,2,1,0:T(8,128)S(1)}, f32[4,8,32,128]{3,2,1,0:T(8,128)S(1)}, u32[]{:S(2)}, u32[]{:S(2)}) collective-permute-start(f32[4,8,32,128]{3,2,1,0:T(8,128)S(1)} %slice_select_fusion.5), channel_id=1, source_target_pairs={{0,32},{32,0},{8,40},{40,8},{16,48},{48,16},{24,56},{56,24},{64,96... | collective-permute-start | bytes 1572872 | tf_op jit(solution)/shard_map/ppermute | solution.py:29
  228.0 19.8 %collective-permute-start.7 = (f32[4,4,32,128]{3,2,1,0:T(8,128)S(1)}, f32[4,4,32,128]{3,2,1,0:T(8,128)S(1)}, u32[]{:S(2)}, u32[]{:S(2)}) collective-permute-start(f32[4,4,32,128]{3,2,1,0:T(8,128)S(1)} %slice_select_fusion.7), channel_id=1, source_target_pairs={{0,64},{64,0},{8,72},{72,8},{16,80},{80,16},{24,88},{88,24},{32,96... | collective-permute-start | bytes 786440 | tf_op jit(solution)/shard_map/ppermute | solution.py:29
  248.0 6.9 %collective-permute-start.8 = (f32[4,2,32,128]{3,2,1,0:T(8,128)S(1)}, f32[4,2,32,128]{3,2,1,0:T(8,128)S(1)}, u32[]{:S(2)}, u32[]{:S(2)}) collective-permute-start(f32[4,2,32,128]{3,2,1,0:T(8,128)S(1)} %slice_select_fusion.9), channel_id=1, source_target_pairs={{0,128},{128,0},{8,136},{136,8},{16,144},{144,16},{24,152},{152,24... | collective-permute-start | bytes 393224 | tf_op jit(solution)/shard_map/ppermute | solution.py:29
  255.0 7.2 %collective-permute-start.9 = (f32[4,1,32,128]{3,2,1,0:T(8,128)S(1)}, f32[4,1,32,128]{3,2,1,0:T(8,128)S(1)}, u32[]{:S(2)}, u32[]{:S(2)}) collective-permute-start(f32[4,1,32,128]{3,2,1,0:T(8,128)S(1)} %slice_select_fusion.11), channel_id=1, source_target_pairs={{0,256},{256,0},{8,264},{264,8},{16,272},{272,16},{24,280},{280,24... | collective-permute-start | bytes 196616 | tf_op jit(solution)/shard_map/ppermute | solution.py:29
where the time goes:
time: 263 us
  waiting for transfers between devices  94.1 us (36%)
  other arithmetic  93.5 us (36%)
  starting transfers between devices  55.8 us (21%)
  local copies, waits for them, and re-layouts  18.8 us (7%)
    ppermute x6, waiting for transfers between devices, swapped(): return lax.ppermute(block, axis, route)  72.5 us
    ppermute x6, starting transfers between devices, swapped(): return lax.ppermute(block, axis, route)  39.6 us
    add x3, other arithmetic, apply_taps(): result + tap_list[offset] * lax.slice_in_dim(array_in, offset, offset + l...  35.2 us
    ppermute x2, waiting for transfers between devices, extended(): before = lax.ppermute(last, axis, up)  17.9 us
    ppermute x2, starting transfers between devices, extended(): before = lax.ppermute(last, axis, up)  12.8 us
    dynamic_slice x8, local copies, waits for them, and re-layouts, composite_planes(): lax.scan(step_fn, start, (jnp.moveaxis(colours, 1, 0), opacity))  12.2 us
    another operation x2, other arithmetic, render_slab(): jnp.stack([jax.nn.sigmoid(2.0 * scaled + 0.5) * weight, (0.5 + 0.4 * jnp....  11.5 us
    add x2, other arithmetic, step_fn(): colour_sum + remain[None] * plane_colour  9.54 us
  transfers between devices with their start and end apart: 10, of which 9 were waited for; matrix products, arithmetic and copies ran while one was open for 0% of the time, Pallas kernels for 0%

commit v1 on v0

v1 whole, which is shorter than its diff:
```python
import functools
import math

import jax
import jax.numpy as jnp
from jax import lax
from jax.experimental import pallas as pl
from jax.experimental.pallas import tpu as pltpu
from jax.sharding import PartitionSpec as P

MESH = pl.DeviceIdType.MESH
F32 = jnp.float32
HALF = math.sqrt(0.48 * 0.48 + 0.6 * 0.6 + 1.64 * 1.64)
ORDER = (0, 1, -1, 2, -2, 3, -3, 4)
NY, NZLO = 8, 4
EARLY = 5


def lanes_of(shape):
    return lax.broadcasted_iota(jnp.int32, shape, 1)


def along_x(x, h):
    lane = lanes_of(x.shape)
    r1 = pltpu.roll(jnp.where(lane == 127, h, x), 1, 1)
    r2 = pltpu.roll(jnp.where(lane >= 126, h, x), 2, 1)
    l1 = pltpu.roll(jnp.where(lane == 0, h, x), 127, 1)
    l2 = pltpu.roll(jnp.where(lane <= 1, h, x), 126, 1)
    gauss = (r2 + l2) + 4.0 * (r1 + l1) + 6.0 * x
    deriv = (l2 - r2) + 2.0 * (l1 - r1)
    return gauss, deriv


def cascade(v):
    for _ in range(3):
        v = [v[k] + v[k + 1] for k in range(len(v) - 1)]
    return v


def shade(s, gz, gy, gx):
    t2 = s * (14.0 / 4096.0)
    e = jnp.exp(-t2)
    sig = 1.0 / (1.0 + e)
    red = 1.0 / (1.0 + math.exp(-0.5) * e)
    op = 0.6 / (1.0 + jnp.exp(jnp.minimum(13.2 - 3.0 * t2, 87.0)))
    inv = lax.rsqrt(gx * gx + gy * gy + (gz * gz + 65536.0))
    dl = 0.48 * gx + 0.6 * gy + 0.64 * gz
    diff = jnp.maximum(dl * inv, 0.0)
    spec = jnp.maximum((dl + gz) * (inv * (1.0 / HALF)), 0.0)
    spec = spec * spec
    spec = spec * spec
    spec = spec * spec
    w = op * (0.25 + 0.6 * diff + 0.35 * spec)
    return op, w, red, 0.1 + 0.8 * sig, e * sig


def kernel(n_depth, n_cols, field, out, fv, wown, wleft, wright, tt, em, rm, re, ht, ug, ud, sf, pim,
           local_sem, wsend, wrecv, msend, mrecv, esend, erecv):
    me = lax.axis_index("depth")
    col = lax.axis_index("cols")
    z, y = me // (2 * NY), me // 2 % NY
    left, right = (col + n_cols - 1) % n_cols, (col + 1) % n_cols
    rows = 2048 // n_depth

    load = pltpu.make_async_copy(field, fv.at[:, pl.ds(8, 2048)], local_sem.at[0])
    load.start()

    barrier = pltpu.get_barrier_semaphore()

    def greet(i, _):
        pl.semaphore_signal(barrier, inc=1, device_id={"depth": (me + i) % n_depth}, device_id_type=MESH)
        return 0

    lax.fori_loop(1, n_depth, greet, 0)
    for other in (left, right):
        pl.semaphore_signal(barrier, inc=1, device_id={"cols": other}, device_id_type=MESH)
    pl.semaphore_wait(barrier, n_depth + 1)

    def peer(o, i):
        return ((z + i // 2) % NZLO) * (2 * NY) + ((y + o + NY) % NY) * 2 + (me + i) % 2

    def main_copy(other, slot):
        return pltpu.make_async_remote_copy(
            src_ref=field.at[:, pl.ds(pl.multiple_of(other * rows, 8), rows)], dst_ref=rm.at[slot],
            send_sem=msend.at[other], recv_sem=mrecv.at[slot],
            device_id={"depth": other}, device_id_type=MESH)

    def edge_copy(other, slot):
        return pltpu.make_async_remote_copy(
            src_ref=em.at[other], dst_ref=re.at[slot],
            send_sem=esend.at[other], recv_sem=erecv.at[slot],
            device_id={"depth": other}, device_id_type=MESH)

    own_main = pltpu.make_async_copy(field.at[:, pl.ds(pl.multiple_of(me * rows, 8), rows)], rm.at[me], local_sem.at[1])
    own_edge = pltpu.make_async_copy(em.at[me], re.at[me], local_sem.at[2])
    own_main.start()

    def each(o, fn):
        lax.fori_loop(1 if o == 0 else 0, 2 * NZLO, lambda i, _: (fn(peer(o, i)), 0)[1], 0)

    for o in ORDER[:EARLY]:
        each(o, lambda other: main_copy(other, me).start())

    load.wait()
    zero = jnp.zeros((8, 128), F32)
    for p in range(2):
        fv[p, 0:8] = zero
        fv[p, 2056:2064] = zero

    def pack(b, _):
        x0 = fv[0, pl.ds(pl.multiple_of(8 + b * 128, 8), 128)]
        x1 = fv[1, pl.ds(pl.multiple_of(8 + b * 128, 8), 128)]
        both = jnp.where(lanes_of(x0.shape) < 4, pltpu.roll(x0, 2, 1), pltpu.roll(x1, 6, 1))
        wown[b] = both.T[0:8]
        return 0

    lax.fori_loop(0, 16, pack, 0)

    to_right = pltpu.make_async_remote_copy(
        src_ref=wown, dst_ref=wleft, send_sem=wsend.at[0], recv_sem=wrecv.at[0],
        device_id={"cols": right}, device_id_type=MESH)
    to_left = pltpu.make_async_remote_copy(
        src_ref=wown, dst_ref=wright, send_sem=wsend.at[1], recv_sem=wrecv.at[1],
        device_id={"cols": left}, device_id_type=MESH)
    to_right.start()
    to_left.start()

    def row_edges(k, _):
        for p in range(2):
            em[k, 4 * p:4 * p + 2] = fv[p, pl.ds(8 + k * rows + rows, 2)]
            em[k, 4 * p + 2:4 * p + 4] = fv[p, pl.ds(8 + k * rows - 2, 2)]
        return 0

    lax.fori_loop(0, n_depth, row_edges, 0)
    tt[0] = zero
    tt[17] = zero
    sub = lax.broadcasted_iota(jnp.int32, (8, 128), 0)
    lane = lanes_of((8, 128))
    from_left = jnp.logical_and(sub % 4 < 2, col > 0)
    from_right = jnp.logical_and(sub % 4 >= 2, col < n_cols - 1)
    to_right.wait()
    to_left.wait()

    def join(b, _):
        tt[b + 1] = jnp.where(from_left, wleft[b], jnp.where(from_right, wright[b], 0.0))
        return 0

    lax.fori_loop(0, 16, join, 0)

    def col_edges(b, _):
        before, here, after = tt[b], tt[b + 1], tt[b + 2]
        for q in range(4):
            turn = (128 - 32 * q) % 128
            main = pltpu.roll(here, turn, 1) if turn else here
            below = pltpu.roll(after, turn, 1) if q == 3 else main
            above = pltpu.roll(before if q == 0 else here, (36 - 32 * q) % 128, 1)
            c = jnp.where(lane < 32, main, jnp.where(lane < 34, below, above))
            c = jnp.where(lane < 36, c, pltpu.roll(c, 4, 1))
            em[4 * b + q, 8:16] = c
        return 0

    lax.fori_loop(0, 16, col_edges, 0)
    own_edge.start()
    for o in ORDER:
        each(o, lambda other: edge_copy(other, me).start())
    for o in ORDER[EARLY:]:
        each(o, lambda other: main_copy(other, me).start())

    for f in range(3):
        for k in (0, 1, 130, 131):
            sf[f, k] = jnp.zeros((32, 128), F32)

    own_edge.wait()
    for o in ORDER:
        each(o, lambda other: edge_copy(other, other).wait_recv())

    def turn_edges(g, _):
        tile = re[pl.ds(g * 16, 16), 8:16].reshape(128, 128)
        ht[g] = tile.T[0:40]
        return 0

    lax.fori_loop(0, NZLO, turn_edges, 0)

    def filter_xy(src):
        group, base = src // 16, src % 16 * 8
        for p in range(2):
            h = pltpu.roll(ht[group, 0:32], (254 - base - 4 * p) % 128, 1)
            g, d = along_x(rm[src, p], h)
            ug[p, 8:40] = g
            ud[p, 8:40] = d
        h = ht[group, 32:40]
        h = jnp.where(sub < 4, pltpu.roll(h, (254 - base) % 128, 1), pltpu.roll(h, (250 - base) % 128, 1))
        g, d = along_x(re[src, 0:8], h)
        for p in range(2):
            ug[p, 40:42] = g[4 * p:4 * p + 2]
            ug[p, 6:8] = g[4 * p + 2:4 * p + 4]
            ud[p, 40:42] = d[4 * p:4 * p + 2]
            ud[p, 6:8] = d[4 * p + 2:4 * p + 4]
        for p in range(2):
            plane = 2 + 2 * src + p
            a, b, c, d, e = (ug[p, 6 + k:38 + k] for k in range(5))
            sf[0, plane] = (a + e) + 4.0 * (b + d) + 6.0 * c
            sf[1, plane] = (e - a) + 2.0 * (d - b)
            a, b, c, d, e = (ud[p, 6 + k:38 + k] for k in range(5))
            sf[2, plane] = (a + e) + 4.0 * (b + d) + 6.0 * c

    def render(grp):
        for j in range(4):
            s, ty, tx = ([sf[f, 4 * grp + k, 8 * j:8 * j + 8] for k in range(8)] for f in range(3))
            s, ty, tx = cascade(s), cascade(ty), cascade(tx)
            for m in range(4):
                op, w, red, green, blue = shade(s[m] + s[m + 1], s[m + 1] - s[m], ty[m] + ty[m + 1], tx[m] + tx[m + 1])
                if m == 0:
                    cr, cg, cb, ca = w * red, w * green, w * blue, op
                else:
                    rest = 1.0 - ca
                    w = rest * w
                    cr, cg, cb, ca = cr + w * red, cg + w * green, cb + w * blue, ca + rest * op
            for i, v in enumerate((cr, cg, cb, ca)):
                pim[grp, i, 8 * j:8 * j + 8] = v

    own_main.wait()

    def arrived(src):
        main_copy(src, src).wait_recv()

    def step(o):
        each(o, arrived)
        lax.fori_loop(0, 2 * NZLO, lambda i, _: (filter_xy(peer(o, i)), 0)[1], 0)

    def show(o):
        lax.fori_loop(0, NZLO, lambda i, _: (render(i * NY + (y + o + NY) % NY), 0)[1], 0)

    step(0)
    for k in (1, 2, 3):
        step(k)
        step(-k)
        if k == 1:
            show(0)
        else:
            show(k - 1)
            show(1 - k)
    step(4)
    show(3)
    show(-3)
    show(4)

    for j in range(4):
        at = pl.ds(8 * j, 8)

        def over(k, acc):
            cr, cg, cb, ca = acc
            rest = 1.0 - ca
            return (cr + rest * pim[k, 0, at], cg + rest * pim[k, 1, at], cb + rest * pim[k, 2, at], ca + rest * pim[k, 3, at])

        for i, v in enumerate(lax.fori_loop(0, n_depth // 2, over, (zero, zero, zero, zero))):
            out[i, at] = v

    to = [main_copy, edge_copy]
    for copy in to:
        for o in ORDER:
            each(o, lambda other: copy(other, me).wait_send())


def solution(mesh):
    n_depth, n_cols = mesh.shape["depth"], mesh.shape["cols"]

    def local(field):
        planes, total, width = field.shape
        rows = total // n_depth
        vmem = lambda *shape: pltpu.VMEM(shape, F32)
        dma = lambda n: pltpu.SemaphoreType.DMA((n,))
        return pl.pallas_call(
            functools.partial(kernel, n_depth, n_cols),
            out_shape=jax.ShapeDtypeStruct((4, rows, width), F32),
            in_specs=[pl.BlockSpec(memory_space=pl.ANY)],
            out_specs=pl.BlockSpec(memory_space=pltpu.VMEM),
            scratch_shapes=[
                vmem(2, total + 16, width),
                vmem(16, 8, 128), vmem(16, 8, 128), vmem(16, 8, 128), vmem(18, 8, 128),
                vmem(n_depth, 16, 128),
                vmem(n_depth, 2, rows, width), vmem(n_depth, 16, 128),
                vmem(4, 40, 128),
                vmem(2, 48, 128), vmem(2, 48, 128),
                vmem(3, 132, rows, width),
                vmem(n_depth // 2, 4, rows, width),
                dma(3), dma(2), dma(2), dma(n_depth), dma(n_depth), dma(n_depth), dma(n_depth),
            ],
            compiler_params=pltpu.CompilerParams(collective_id=0, has_side_effects=True, vmem_limit_bytes=48 << 20),
        )(field)

    return jax.shard_map(local, mesh=mesh, in_specs=(P("depth", None, "cols"),), out_specs=P(None, "depth", "cols"), check_vma=False)
```

time: 263 us -> 114 us (0.43)
  the two profiles are of different devices: /device:TPU:6 before, /device:TPU:175 now
where the time goes in v1:
time: 114 us
  Pallas kernels  112 us (98%)
  local copies, waits for them, and re-layouts  2.22 us (2%)
    pallas_call x1, Pallas kernels, local(): pl.pallas_call(functools.partial(kernel, n_depth, n_cols), out_shape=jax....  112 us

profile of v1, /device:TPU:175, one launch (start us, length us, event | category | flops | bytes accessed | tf_op | source)
XLA Modules:
  0.0 114.3 jit_solution(5917533714171770292)
XLA Ops:
  0.0 0.0 copy-start
  0.0 1.6 %copy-done = f32[2,2048,128]{2,1,0:T(8,128)S(1)} copy-done((f32[2,2048,128]{2,1,0:T(8,128)S(1)}, f32[2,2048,128]{2,1,0:T(8,128)}, u32[]{:S(2)}) %copy-start) | copy-done | bytes 2097176
  1.6 112.0 %shard_map.17 = f32[4,32,128]{2,1,0:T(8,128)S(1)} custom-call(f32[2,2048,128]{2,1,0:T(8,128)S(1)} %copy-done), custom_call_target="tpu_custom_call" | custom-call | tf_op jit(solution)/shard_map/pallas_call | solution.py:273
  113.6 0.6 copy.3
Async XLA Ops:
  0.0 1.6 %copy-start = (f32[2,2048,128]{2,1,0:T(8,128)S(1)}, f32[2,2048,128]{2,1,0:T(8,128)}, u32[]{:S(2)}) copy-start(f32[2,2048,128]{2,1,0:T(8,128)} %field.1) | copy-start | bytes 6291460

commit v2 on v1

v2 whole, which is shorter than its diff:
```python
import functools
import math

import jax
import jax.numpy as jnp
from jax import lax
from jax.experimental import pallas as pl
from jax.experimental.pallas import tpu as pltpu
from jax.sharding import PartitionSpec as P

MESH = pl.DeviceIdType.MESH
F32 = jnp.float32
HALF = math.sqrt(0.48 * 0.48 + 0.6 * 0.6 + 1.64 * 1.64)
ORDER = (0, 1, -1, 2, -2, 3, -3, 4)
NY, NZLO = 8, 4
TURNS = (2, 3, 1, 0)
SENT = [(o, k) for d in (1, 2, 3) for k in TURNS for o in (d, -d)] + [(4, k) for k in TURNS]
EARLY = 16


def lanes_of(shape):
    return lax.broadcasted_iota(jnp.int32, shape, 1)


def along_x(x, h):
    lane = lanes_of(x.shape)
    r1 = pltpu.roll(jnp.where(lane == 127, h, x), 1, 1)
    r2 = pltpu.roll(jnp.where(lane >= 126, h, x), 2, 1)
    l1 = pltpu.roll(jnp.where(lane == 0, h, x), 127, 1)
    l2 = pltpu.roll(jnp.where(lane <= 1, h, x), 126, 1)
    gauss = (r2 + l2) + 4.0 * (r1 + l1) + 6.0 * x
    deriv = (l2 - r2) + 2.0 * (l1 - r1)
    return gauss, deriv


def cascade(v):
    for _ in range(3):
        v = [v[k] + v[k + 1] for k in range(len(v) - 1)]
    return v


def shade(s, gz, gy, gx):
    t2 = s * (14.0 / 4096.0)
    e = jnp.exp(-t2)
    sig = 1.0 / (1.0 + e)
    red = 1.0 / (1.0 + math.exp(-0.5) * e)
    op = 0.6 / (1.0 + jnp.exp(jnp.minimum(13.2 - 3.0 * t2, 87.0)))
    inv = lax.rsqrt(gx * gx + gy * gy + (gz * gz + 65536.0))
    dl = 0.48 * gx + 0.6 * gy + 0.64 * gz
    diff = jnp.maximum(dl * inv, 0.0)
    spec = jnp.maximum((dl + gz) * (inv * (1.0 / HALF)), 0.0)
    spec = spec * spec
    spec = spec * spec
    spec = spec * spec
    w = op * (0.25 + 0.6 * diff + 0.35 * spec)
    return op, w, red, 0.1 + 0.8 * sig, e * sig


def kernel(n_depth, n_cols, field, out, fv, wlast, wfirst, wleft, wright, tt, em, e1, e2, e3, a1, a2, a3, ht, ug, ud, sf, pim,
           local_sem, wsend, wrecv, s1, m1, s2, m2, s3, m3, es1, er1, es2, er2, es3, er3):
    me = lax.axis_index("depth")
    col = lax.axis_index("cols")
    z, y, core = me // (2 * NY), me // 2 % NY, me % 2
    left, right = (col + n_cols - 1) % n_cols, (col + 1) % n_cols
    block, span = 64, NY * 64

    load = pltpu.make_async_copy(field, fv.at[:, pl.ds(8, NZLO * span)], local_sem.at[0])
    load.start()

    def depth_of(zz, yy, cc):
        return {"depth": zz * (2 * NY) + yy * 2 + cc}

    def copy(src, dst, send, recv, where):
        return pltpu.make_async_remote_copy(
            src_ref=src, dst_ref=dst, send_sem=send, recv_sem=recv, device_id=where, device_id_type=MESH)

    def at_y(o):
        return (y + o + NY) % NY

    def at_z(k):
        return (z + k + NZLO) % NZLO

    partner = depth_of(z, y, 1 - core)
    barrier = pltpu.get_barrier_semaphore()

    def greet(where):
        pl.semaphore_signal(barrier, inc=1, device_id=where, device_id_type=MESH)

    for o in ORDER[1:]:
        greet(depth_of(z, at_y(o), core))
    for k in range(1, NZLO):
        greet(depth_of(at_z(k), y, core))
    greet(partner)
    greet({"cols": left})
    greet({"cols": right})
    pl.semaphore_wait(barrier, NY - 1 + NZLO - 1 + 3)

    def rows_of(zz, yy):
        return fv.at[:, pl.ds(pl.multiple_of(8 + zz * span + yy * block, 8), block)]

    def hop1(o, k):
        yy = at_y(o)
        dst = a2.at[z, y] if k == 0 else a1.at[y, k - 1]
        return copy(rows_of(at_z(k), yy), dst, s1.at[yy * NZLO + k], m1.at[y * NZLO + k], depth_of(z, yy, core))

    def got1(o, k):
        yy = at_y(o)
        dst = a2.at[z, yy] if k == 0 else a1.at[yy, k - 1]
        return copy(rows_of(at_z(k), yy), dst, s1.at[yy * NZLO + k], m1.at[yy * NZLO + k], depth_of(z, yy, core))

    def hop2(o, k):
        yy, zz = at_y(o), at_z(k)
        src = rows_of(zz, yy) if o == 0 else a1.at[yy, k - 1]
        return copy(src, a2.at[z, yy], s2.at[yy * NZLO + k], m2.at[z * NY + yy], depth_of(zz, y, core))

    def got2(o, k):
        yy, zz = at_y(o), at_z(-k)
        return copy(a2.at[zz, yy], a2.at[zz, yy], s2.at[yy * NZLO + k], m2.at[zz * NY + yy], depth_of(zz, y, core))

    def hop3(o, k):
        yy, zz = at_y(o), at_z(-k)
        src = a2.at[zz, yy, :, pl.ds(pl.multiple_of(24 * (1 - core), 8), 40)]
        return copy(src, a3.at[zz, yy], s3.at[zz * NY + yy], m3.at[zz * NY + yy], partner)

    load.wait()
    own = pltpu.make_async_copy(rows_of(z, y), a2.at[z, y], local_sem.at[1])
    own.start()
    for o, k in SENT[:EARLY]:
        hop1(o, k).start()
    for k in TURNS[:-1]:
        hop2(0, k).start()
    zero = jnp.zeros((8, 128), F32)
    for p in range(2):
        fv[p, 0:8] = zero
        fv[p, 2056:2064] = zero
    own.wait()
    hop3(0, 0).start()

    def edges_of(b):
        x0 = fv[0, pl.ds(pl.multiple_of(8 + b * 128, 8), 128)]
        x1 = fv[1, pl.ds(pl.multiple_of(8 + b * 128, 8), 128)]
        both = jnp.where(lanes_of(x0.shape) < 4, pltpu.roll(x0, 2, 1), pltpu.roll(x1, 6, 1))
        return both.T[0:8]

    sub = lax.broadcasted_iota(jnp.int32, (8, 128), 0)
    lane = lanes_of((8, 128))
    is_last = sub % 4 < 2

    def pack(b, _):
        even, odd = edges_of(2 * b), edges_of(2 * b + 1)
        wlast[b] = jnp.where(is_last, even, pltpu.roll(odd, 2, 0))
        wfirst[b] = jnp.where(is_last, pltpu.roll(odd, 6, 0), even)
        return 0

    lax.fori_loop(0, 8, pack, 0)
    to_right = copy(wlast, wleft, wsend.at[0], wrecv.at[0], {"cols": right})
    to_left = copy(wfirst, wright, wsend.at[1], wrecv.at[1], {"cols": left})
    to_right.start()
    to_left.start()

    def row_edges(k, _):
        yy, zz = k // NZLO, k % NZLO
        first = 8 + zz * span + yy * block
        for p in range(2):
            em[yy, zz, 4 * p:4 * p + 2] = fv[p, pl.ds(first + block, 2)]
            em[yy, zz, 4 * p + 2:4 * p + 4] = fv[p, pl.ds(first - 2, 2)]
        return 0

    lax.fori_loop(0, NY * NZLO, row_edges, 0)
    for f in range(3):
        for k in (0, 1, 130, 131):
            sf[f, k] = jnp.zeros((32, 128), F32)
    tt[0] = zero
    tt[17] = zero
    to_right.wait()
    to_left.wait()

    def join(b, _):
        wl = jnp.where(col > 0, wleft[b], 0.0)
        wr = jnp.where(col < n_cols - 1, wright[b], 0.0)
        tt[2 * b + 1] = jnp.where(is_last, wl, wr)
        tt[2 * b + 2] = jnp.where(is_last, pltpu.roll(wl, 6, 0), pltpu.roll(wr, 2, 0))
        return 0

    lax.fori_loop(0, 8, join, 0)

    def col_edges(b, _):
        before, here, after = tt[b], tt[b + 1], tt[b + 2]
        for q in range(2):
            main = pltpu.roll(here, 64, 1) if q else here
            below = pltpu.roll(after, 64, 1) if q else here
            above = pltpu.roll(here if q else before, 4 + 64 * (1 - q), 1)
            c = jnp.where(lane < 64, main, jnp.where(lane < 66, below, above))
            c = jnp.where(lane < 68, c, pltpu.roll(c, 4, 1))
            k = 2 * b + q
            em[k % NY, k // NY, 8:16] = c
        return 0

    lax.fori_loop(0, 16, col_edges, 0)

    def edge1(o, mine):
        yy = at_y(o)
        slot = y if mine else yy
        return copy(em.at[yy], e1.at[slot], es1.at[yy], er1.at[slot], depth_of(z, yy, core))

    def edge2(k, mine):
        zz = at_z(k) if mine else at_z(-k)
        slot = z if mine else zz
        return copy(e1.at[:, zz], e2.at[slot], es2.at[k], er2.at[slot], depth_of(zz, y, core))

    edge3 = copy(e2, e3, es3.at[0], er3.at[0], partner)

    for o in ORDER[1:]:
        edge1(o, True).start()
    for o, k in SENT[EARLY:]:
        hop1(o, k).start()
    e1[y] = em[y]

    def filter_xy(zz, yy, tile, edges, src_core, base):
        h = ht[zz, 64:72]
        h = jnp.where(sub < 4, pltpu.roll(h, (254 - base) % 128, 1), pltpu.roll(h, (250 - base) % 128, 1))
        g, d = along_x(edges[zz, yy, 0:8], h)
        for p in range(2):
            ug[p, 40:42] = g[4 * p:4 * p + 2]
            ug[p, 6:8] = g[4 * p + 2:4 * p + 4]
            ud[p, 40:42] = d[4 * p:4 * p + 2]
            ud[p, 6:8] = d[4 * p + 2:4 * p + 4]
        at = pl.ds(pl.multiple_of(8 - 8 * core, 8), 40)
        for p in range(2):
            h = pltpu.roll(ht[zz, pl.ds(pl.multiple_of(24 * core, 8), 40)], (254 - base - 4 * p) % 128, 1)
            g, d = along_x(tile(zz, yy, p), h)
            ug[p, at] = g
            ud[p, at] = d
        for p in range(2):
            plane = 2 + 2 * (2 * (NY * zz + yy) + src_core) + p
            a, b, c, d, e = (ug[p, 6 + k:38 + k] for k in range(5))
            sf[0, plane] = (a + e) + 4.0 * (b + d) + 6.0 * c
            sf[1, plane] = (e - a) + 2.0 * (d - b)
            a, b, c, d, e = (ud[p, 6 + k:38 + k] for k in range(5))
            sf[2, plane] = (a + e) + 4.0 * (b + d) + 6.0 * c

    def own_tile(zz, yy, p):
        return a2[zz, yy, p, pl.ds(pl.multiple_of(24 * core, 8), 40)]

    def other_tile(zz, yy, p):
        return a3[zz, yy, p]

    def render(grp):
        for j in range(4):
            s, ty, tx = ([sf[f, 4 * grp + k, 8 * j:8 * j + 8] for k in range(8)] for f in range(3))
            s, ty, tx = cascade(s), cascade(ty), cascade(tx)
            for m in range(4):
                op, w, red, green, blue = shade(s[m] + s[m + 1], s[m + 1] - s[m], ty[m] + ty[m + 1], tx[m] + tx[m + 1])
                if m == 0:
                    cr, cg, cb, ca = w * red, w * green, w * blue, op
                else:
                    rest = 1.0 - ca
                    w = rest * w
                    cr, cg, cb, ca = cr + w * red, cg + w * green, cb + w * blue, ca + rest * op
            for i, v in enumerate((cr, cg, cb, ca)):
                pim[grp, i, 8 * j:8 * j + 8] = v

    def pass_on(o, k):
        got1(o, k).wait_recv()
        (hop2 if k else hop3)(o, k).start()

    def pass_over(o, k):
        got2(o, k).wait_recv()
        hop3(o, k).start()

    def forward(o):
        for k in TURNS:
            pass_on(o, k)

    def share(o):
        for k in TURNS[:-1]:
            pass_over(o, k)

    def filter_chip(zz, yy):
        filter_xy(zz, yy, own_tile, e2, core, 8 * yy)
        filter_xy(zz, yy, other_tile, e3, 1 - core, 64 + 8 * yy)

    def step(o, low=0, high=NZLO):
        for i in range(low, high):
            hop3(o, -i).wait_recv()
        lax.fori_loop(low, high, lambda i, _: (filter_chip(at_z(i), at_y(o)), 0)[1], 0)

    def show(o, low=0, high=NZLO):
        lax.fori_loop(low, high, lambda i, _: (render((z + i) % NZLO * NY + at_y(o)), 0)[1], 0)

    forward(1)
    share(0)
    forward(-1)
    share(1)
    forward(2)
    share(-1)
    forward(-2)
    share(2)
    for o in ORDER[1:]:
        edge1(o, False).wait_recv()
    for k in range(1, NZLO):
        edge2(k, True).start()
    for i in range(NY):
        e2[z, i] = e1[i, z]
    share(-2)
    for k in range(1, NZLO):
        edge2(k, False).wait_recv()
    edge3.start()
    edge3.wait_recv()

    def turn_edges(g, _):
        tile = jnp.concatenate([e2[g, :, 8:16].reshape(64, 128), e3[g, :, 8:16].reshape(64, 128)], 0)
        ht[g] = tile.T[0:72]
        return 0

    lax.fori_loop(0, NZLO, turn_edges, 0)

    def both_ways(act, k):
        act(3, k)
        act(-3, k)

    step(0)
    both_ways(pass_on, 2)
    step(1)
    both_ways(pass_on, 3)
    step(-1)
    both_ways(pass_over, 2)
    show(0)
    both_ways(pass_on, 1)
    both_ways(pass_over, 3)
    step(2)
    step(-2)
    both_ways(pass_on, 0)
    both_ways(pass_over, 1)
    show(1)
    show(-1)
    for o in ORDER[1:5]:
        edge1(o, True).wait_send()
        for k in TURNS:
            hop1(o, k).wait_send()
    for o in ORDER[:5]:
        for k in TURNS[:-1]:
            hop2(o, k).wait_send()
        for k in TURNS:
            hop3(o, k).wait_send()
    for k in range(1, NZLO):
        edge2(k, True).wait_send()
    edge3.wait_send()

    def finish(k):
        hop3(4, k).wait_recv()
        zz, yy = at_z(-k), at_y(4)
        filter_chip(zz, yy)
        groups = NY * NZLO
        lax.fori_loop(0, 3, lambda i, _: (render((zz * NY + yy + i - 1 + groups) % groups), 0)[1], 0)

    step(3)
    pass_on(4, 2)
    show(2)
    pass_on(4, 3)
    step(-3)
    pass_over(4, 2)
    pass_on(4, 1)
    show(-2)
    pass_over(4, 3)
    pass_on(4, 0)
    finish(2)
    pass_over(4, 1)
    finish(3)
    finish(0)
    finish(1)

    def over(k, acc):
        cr, cg, cb, ca = acc
        rest = 1.0 - ca
        return (cr + rest * pim[k, 0], cg + rest * pim[k, 1], cb + rest * pim[k, 2], ca + rest * pim[k, 3])

    blank = jnp.zeros((32, 128), F32)
    for i, v in enumerate(lax.fori_loop(0, n_depth // 2, over, (blank, blank, blank, blank))):
        out[i] = v

    for o in ORDER[5:]:
        edge1(o, True).wait_send()
        for k in TURNS:
            hop1(o, k).wait_send()
        for k in TURNS[:-1]:
            hop2(o, k).wait_send()
        for k in TURNS:
            hop3(o, k).wait_send()


def solution(mesh):
    n_depth, n_cols = mesh.shape["depth"], mesh.shape["cols"]

    def local(field):
        planes, total, width = field.shape
        rows = total // n_depth
        vmem = lambda *shape: pltpu.VMEM(shape, F32)
        dma = lambda n: pltpu.SemaphoreType.DMA((n,))
        return pl.pallas_call(
            functools.partial(kernel, n_depth, n_cols),
            out_shape=jax.ShapeDtypeStruct((4, rows, width), F32),
            in_specs=[pl.BlockSpec(memory_space=pltpu.HBM)],
            out_specs=pl.BlockSpec(memory_space=pltpu.VMEM),
            scratch_shapes=[
                vmem(2, total + 16, width),
                vmem(8, 8, 128), vmem(8, 8, 128), vmem(8, 8, 128), vmem(8, 8, 128), vmem(18, 8, 128),
                vmem(NY, NZLO, 16, 128), vmem(NY, NZLO, 16, 128), vmem(NZLO, NY, 16, 128), vmem(NZLO, NY, 16, 128),
                vmem(NY, NZLO - 1, 2, 64, 128), vmem(NZLO, NY, 2, 64, 128), vmem(NZLO, NY, 2, 40, 128),
                vmem(NZLO, 72, 128),
                vmem(2, 48, 128), vmem(2, 48, 128),
                vmem(3, 132, rows, width),
                vmem(n_depth // 2, 4, rows, width),
                dma(2), dma(2), dma(2),
                dma(32), dma(32), dma(32), dma(32), dma(32), dma(32),
                dma(NY), dma(NY), dma(NZLO), dma(NZLO), dma(1), dma(1),
            ],
            compiler_params=pltpu.CompilerParams(collective_id=0, has_side_effects=True, vmem_limit_bytes=63 << 20),
        )(field)

    return jax.shard_map(local, mesh=mesh, in_specs=(P("depth", None, "cols"),), out_specs=P(None, "depth", "cols"), check_vma=False)
```

time: 114 us -> 90.2 us (0.79)
  the two profiles are of different devices: /device:TPU:175 before, /device:TPU:1 now
where the time goes in v2:
time: 90.2 us; the launch traced here: 90 us
  Pallas kernels  88.6 us (98%)
  local copies, waits for them, and re-layouts  1.47 us (2%)
    pallas_call x1, Pallas kernels, local(): pl.pallas_call(functools.partial(kernel, n_depth, n_cols), out_shape=jax....  88.6 us

profile of v2, /device:TPU:1, one launch (start us, length us, event | category | flops | bytes accessed | tf_op | source)
XLA Modules:
  0.0 90.0 jit_solution(8909233941445373091)
XLA Ops:
  0.0 88.6 %shard_map.17 = f32[4,32,128]{2,1,0:T(8,128)} custom-call(f32[2,2048,128]{2,1,0:T(8,128)} %field.1), custom_call_target="tpu_custom_call" | custom-call | tf_op jit(solution)/shard_map/pallas_call | solution.py:400
  88.6 1.5 %copy.3 = f32[4,32,128]{2,1,0:T(8,128)} copy(f32[4,32,128]{2,1,0:T(8,128)} %shard_map.17) | data formatting | bytes 131072

commit v3 on v2

--- a/solution.py
+++ b/solution.py
@@ -15,7 +15,7 @@
 NY, NZLO = 8, 4
 TURNS = (2, 3, 1, 0)
 SENT = [(o, k) for d in (1, 2, 3) for k in TURNS for o in (d, -d)] + [(4, k) for k in TURNS]
-EARLY = 16
+EARLY = 12
 
 
 def lanes_of(shape):
@@ -127,15 +127,10 @@
     own.start()
     for o, k in SENT[:EARLY]:
         hop1(o, k).start()
-    for k in TURNS[:-1]:
-        hop2(0, k).start()
     zero = jnp.zeros((8, 128), F32)
     for p in range(2):
         fv[p, 0:8] = zero
         fv[p, 2056:2064] = zero
-    own.wait()
-    hop3(0, 0).start()
-
     def edges_of(b):
         x0 = fv[0, pl.ds(pl.multiple_of(8 + b * 128, 8), 128)]
         x1 = fv[1, pl.ds(pl.multiple_of(8 + b * 128, 8), 128)]
@@ -157,6 +152,10 @@
     to_left = copy(wfirst, wright, wsend.at[1], wrecv.at[1], {"cols": left})
     to_right.start()
     to_left.start()
+    for k in TURNS[:-1]:
+        hop2(0, k).start()
+    own.wait()
+    hop3(0, 0).start()
 
     def row_edges(k, _):
         yy, zz = k // NZLO, k % NZLO
@@ -292,20 +291,20 @@
     share(0)
     forward(-1)
     share(1)
-    forward(2)
-    share(-1)
-    forward(-2)
-    share(2)
     for o in ORDER[1:]:
         edge1(o, False).wait_recv()
     for k in range(1, NZLO):
         edge2(k, True).start()
     for i in range(NY):
         e2[z, i] = e1[i, z]
-    share(-2)
+    forward(2)
+    share(-1)
     for k in range(1, NZLO):
         edge2(k, False).wait_recv()
     edge3.start()
+    forward(-2)
+    share(2)
+    share(-2)
     edge3.wait_recv()
 
     def turn_edges(g, _):
@@ -315,25 +314,16 @@
 
     lax.fori_loop(0, NZLO, turn_edges, 0)
 
-    def both_ways(act, k):
-        act(3, k)
-        act(-3, k)
-
-    step(0)
-    both_ways(pass_on, 2)
-    step(1)
-    both_ways(pass_on, 3)
-    step(-1)
-    both_ways(pass_over, 2)
-    show(0)
-    both_ways(pass_on, 1)
-    both_ways(pass_over, 3)
-    step(2)
-    step(-2)
-    both_ways(pass_on, 0)
-    both_ways(pass_over, 1)
-    show(1)
-    show(-1)
+    first, second, third, last = TURNS
+    ticks = [(act, o, k) for act, k in ((pass_on, first), (pass_on, second), (pass_over, first), (pass_on, third),
+                                        (pass_over, second), (pass_on, last), (pass_over, third)) for o in (3, -3)]
+    work = [(act, o, i) for act, o in ((step, 0), (step, 1), (step, -1), (show, 0), (step, 2), (step, -2), (show, 1),
+                                       (show, -1)) for i in (0, 2)]
+    for n, (act, o, i) in enumerate(work):
+        act(o, i, i + 2)
+        if n >= 2:
+            pass_piece, oo, k = ticks[n - 2]
+            pass_piece(oo, k)
     for o in ORDER[1:5]:
         edge1(o, True).wait_send()
         for k in TURNS:
@@ -354,21 +344,24 @@
         groups = NY * NZLO
         lax.fori_loop(0, 3, lambda i, _: (render((zz * NY + yy + i - 1 + groups) % groups), 0)[1], 0)
 
-    step(3)
-    pass_on(4, 2)
-    show(2)
-    pass_on(4, 3)
-    step(-3)
-    pass_over(4, 2)
-    pass_on(4, 1)
+    step(3, 0, 2)
+    pass_on(4, first)
+    step(3, 2, 4)
+    show(2, 0, 2)
+    pass_on(4, second)
+    show(2, 2, 4)
+    pass_over(4, first)
+    step(-3, 0, 2)
+    pass_on(4, third)
+    step(-3, 2, 4)
+    pass_over(4, second)
     show(-2)
-    pass_over(4, 3)
+    finish(first)
     pass_on(4, 0)
-    finish(2)
-    pass_over(4, 1)
-    finish(3)
+    pass_over(4, third)
+    finish(second)
     finish(0)
-    finish(1)
+    finish(third)
 
     def over(k, acc):
         cr, cg, cb, ca = acc

time: 90.2 us -> 86.4 us (0.958)
  the two profiles are of different devices: /device:TPU:1 before, /device:TPU:24 now
where the time goes in v3:
time: 86.4 us; the launch traced here: 86.3 us
  Pallas kernels  84.8 us (98%)
  local copies, waits for them, and re-layouts  1.47 us (2%)
    pallas_call x1, Pallas kernels, local(): pl.pallas_call(functools.partial(kernel, n_depth, n_cols), out_shape=jax....  84.8 us

profile of v3, /device:TPU:24, one launch (start us, length us, event | category | flops | bytes accessed | tf_op | source)
XLA Modules:
  0.0 86.3 jit_solution(3820522049797218505)
XLA Ops:
  0.0 84.8 %shard_map.17 = f32[4,32,128]{2,1,0:T(8,128)} custom-call(f32[2,2048,128]{2,1,0:T(8,128)} %field.1), custom_call_target="tpu_custom_call" | custom-call | tf_op jit(solution)/shard_map/pallas_call | solution.py:393
  84.8 1.5 %copy.3 = f32[4,32,128]{2,1,0:T(8,128)} copy(f32[4,32,128]{2,1,0:T(8,128)} %shard_map.17) | data formatting | bytes 131072

commit v4 on v3

--- a/solution.py
+++ b/solution.py
@@ -305,6 +305,15 @@
     forward(-2)
     share(2)
     share(-2)
+    for o in (1, -1):
+        edge1(o, True).wait_send()
+        for k in TURNS:
+            hop1(o, k).wait_send()
+    for o in (0, 1, -1):
+        for k in TURNS[:-1]:
+            hop2(o, k).wait_send()
+    for k in TURNS:
+        hop3(0, k).wait_send()
     edge3.wait_recv()
 
     def turn_edges(g, _):
@@ -324,19 +333,6 @@
         if n >= 2:
             pass_piece, oo, k = ticks[n - 2]
             pass_piece(oo, k)
-    for o in ORDER[1:5]:
-        edge1(o, True).wait_send()
-        for k in TURNS:
-            hop1(o, k).wait_send()
-    for o in ORDER[:5]:
-        for k in TURNS[:-1]:
-            hop2(o, k).wait_send()
-        for k in TURNS:
-            hop3(o, k).wait_send()
-    for k in range(1, NZLO):
-        edge2(k, True).wait_send()
-    edge3.wait_send()
-
     def finish(k):
         hop3(4, k).wait_recv()
         zz, yy = at_z(-k), at_y(4)
@@ -357,6 +353,18 @@
     pass_over(4, second)
     show(-2)
     finish(first)
+    for o in (2, -2):
+        edge1(o, True).wait_send()
+        for k in TURNS:
+            hop1(o, k).wait_send()
+        for k in TURNS[:-1]:
+            hop2(o, k).wait_send()
+    for k in range(1, NZLO):
+        edge2(k, True).wait_send()
+    edge3.wait_send()
+    for o in ORDER[1:5]:
+        for k in TURNS:
+            hop3(o, k).wait_send()
     pass_on(4, 0)
     pass_over(4, third)
     finish(second)

time: 86.4 us -> 86.5 us (level)
  no operation moved by 1% of the time
where the time goes in v4:
time: 86.5 us; the launch traced here: 86.3 us
  Pallas kernels  84.8 us (98%)
  local copies, waits for them, and re-layouts  1.47 us (2%)
    pallas_call x1, Pallas kernels, local(): pl.pallas_call(functools.partial(kernel, n_depth, n_cols), out_shape=jax....  84.8 us

profile of v4, /device:TPU:24, one launch (start us, length us, event | category | flops | bytes accessed | tf_op | source)
XLA Modules:
  0.0 86.3 jit_solution(6088479201362213351)
XLA Ops:
  0.0 84.8 %shard_map.17 = f32[4,32,128]{2,1,0:T(8,128)} custom-call(f32[2,2048,128]{2,1,0:T(8,128)} %field.1), custom_call_target="tpu_custom_call" | custom-call | tf_op jit(solution)/shard_map/pallas_call | solution.py:401
  84.8 1.5 %copy.3 = f32[4,32,128]{2,1,0:T(8,128)} copy(f32[4,32,128]{2,1,0:T(8,128)} %shard_map.17) | data formatting | bytes 131072
